TPU v7x, 256 devices: a whole 4x4x8 slice. The times are simulated.
256 devices in a mesh: gx: 32 (over y, z), gy: 8 (over x, core).
Axes of the slice: x: 4, y: 4, z: 8, core: 2. Of those that a mesh axis runs over, the one named last changes fastest.
Arguments:
- densities: bfloat16 [24576, 32, 128], P(('gx', 'gy')), may hold values from -6 to 6
- geometry: float32 [24576, 7, 128], P(('gx', 'gy')), as said below
- near_ids: int32 [24576, 8], P(('gx', 'gy')), may hold values from 0 to 24575, as said below
- basis_in: bfloat16 [24576, 64, 128], P(('gx', 'gy')), may hold values from -0.5 to 0.5
- basis_out: bfloat16 [24576, 64, 128], P(('gx', 'gy')), may hold values from -0.75 to 0.75
- leaf_up: bfloat16 [24576, 64, 64], P(('gx', 'gy')), may hold values from -0.078125 to 0.078125
- leaf_down: bfloat16 [24576, 64, 64], P(('gx', 'gy')), may hold values from -0.75 to 0.75
- leaf_coupling: bfloat16 [24576, 6, 64, 64], P(('gx', 'gy')), may hold values from -0.3125 to 0.3125
- leaf_far: int32 [24576, 6], P(('gx', 'gy')), may hold values from 0 to 24575, as said below
- leaf_count: int32 [24576], P(('gx', 'gy')), may hold values from 1 to 6, as said below
- cluster_up: bfloat16 [256, 64, 64], P(('gx', 'gy')), may hold values from -0.25 to 0.25
- cluster_down: bfloat16 [256, 64, 64], P(('gx', 'gy')), may hold values from -0.75 to 0.75
- cluster_coupling: bfloat16 [256, 6, 64, 64], P(('gx', 'gy')), may hold values from -0.3125 to 0.3125
- cluster_far: int32 [256, 6], P(('gx', 'gy')), may hold values from 0 to 255, as said below
- group_up: bfloat16 [32, 64, 64], replicated, may hold values from -0.375 to 0.375
- group_down: bfloat16 [32, 64, 64], P('gx'), may hold values from -0.75 to 0.75
- group_coupling: bfloat16 [32, 6, 64, 64], P('gx'), may hold values from -0.3125 to 0.3125
- group_far: int32 [32, 6], P('gx'), may hold values from 0 to 31, as said below
- root_coupling: bfloat16 [8, 8, 64, 64], replicated, may hold values from -0.25 to 0.25
Outputs:
- potential: float32 [24576, 32, 128], P(('gx', 'gy'))
Inputs may be any that keep to these rules, and one draw needn't show every extreme that they name: `near_ids`: row l names 8 different leaves of a window of 9 consecutive leaves that contains l, centred on l where the ends allow. `leaf_far`: row l names 6 different leaves held by l's device or its two neighbours in leaf order, none within 4 leaves of l; only the first leaf_count[l] entries are used. `leaf_count`: every device holds a leaf with 6. `cluster_far`: row u names 6 different level-two clusters other than u, of u's group or the two groups beside it. `group_far`: row g names 6 different level-one clusters other than g. `geometry`: rows 0 to 2 hold a panel's centre, rows 3 to 5 its unit normal, row 6 its area, from 0.25 to 2.
All inputs are finite; a program needn't handle non-finite values.
Results may differ from a plain program's by a relative error of at most 0.012.
Values may be sent and summed in bfloat16 or wider, within the bound.
A program may use at most 128 MiB of HBM per device.

v0:
```python
import math
import jax
import jax.numpy as jnp
from jax import lax
from jax.sharding import PartitionSpec as P

REACH = 4
BRANCH = 4
four_pi = 4.0 * math.pi
leaf_block = 8


def padded(cells, sides, width):
    for axis, dim in sides:
        count = lax.axis_size(axis)
        ends = count - 1
        head = lax.slice_in_dim(cells, 0, width, axis=dim)
        tail = lax.slice_in_dim(cells, cells.shape[dim] - width, cells.shape[dim], axis=dim)
        cells = jnp.concatenate(
            [
                lax.ppermute(tail, axis, [(i, (i + 1) % count) for i in range(ends)]),
                cells,
                lax.ppermute(head, axis, [((i + 1) % count, i) for i in range(ends)]),
            ],
            axis=dim,
        )
    return cells


def near_kernel(target, source):
    offsets = [
        target[:, coord_id, :, None, None] - source[:, None, :, coord_id, :]
        for coord_id in range(3)
    ]
    distance = offsets[0] * offsets[0] + offsets[1] * offsets[1] + offsets[2] * offsets[2]
    facing = (
        source[:, None, :, 3, :] * offsets[0]
        + source[:, None, :, 4, :] * offsets[1]
        + source[:, None, :, 5, :] * offsets[2]
    )
    panel_area = source[:, None, :, 6, :]
    spread = distance + panel_area
    return panel_area * facing / (four_pi * spread * jnp.sqrt(spread))


def on_device(
    densities,
    geometry,
    near_ids,
    basis_in,
    basis_out,
    leaf_up,
    leaf_down,
    leaf_coupling,
    leaf_far,
    leaf_count,
    cluster_up,
    cluster_down,
    cluster_coupling,
    cluster_far,
    group_up,
    group_down,
    group_coupling,
    group_far,
    root_coupling,
):
    wide = jnp.float32
    narrow = jnp.bfloat16
    leaves = densities.shape[0]
    coeff_order = basis_in.shape[1]
    columns = densities.shape[1]
    flat = coeff_order * columns
    first_leaf = lax.axis_index(("gx", "gy")) * leaves
    gx_index = lax.axis_index("gx")
    group_size = lax.axis_size("gy")
    groups = lax.axis_size("gx")
    leaf_coeffs = jnp.einsum(
        "lkm,lrm->lkr", basis_in, densities, preferred_element_type=wide
    ).astype(narrow)
    mid_coeffs = jnp.einsum(
        "lik,lkr->ir", leaf_up, leaf_coeffs, preferred_element_type=wide
    ).astype(narrow)
    mid_term = jnp.dot(cluster_up[0], mid_coeffs, preferred_element_type=wide).reshape(1, flat)
    mid_flat = mid_coeffs.reshape(1, flat)
    siblings = lax.all_gather(mid_flat, "gy", axis=0, tiled=True)
    group_sum = lax.psum(mid_term, "gy")
    nearby = padded(siblings, (("gx", 0),), group_size)
    mid_picked = jnp.take(nearby, cluster_far[0] - (gx_index - 1) * group_size, axis=0)
    top_coeffs = lax.all_gather(group_sum.astype(narrow), "gx", axis=0, tiled=True)
    top_block = top_coeffs.reshape(groups, coeff_order, columns)
    root_terms = jnp.einsum("gik,gkr->gir", group_up, top_block, preferred_element_type=wide)
    root_coeffs = jnp.sum(
        root_terms.reshape(groups // BRANCH, BRANCH, coeff_order, columns), axis=1
    ).astype(narrow)
    root_row = lax.dynamic_index_in_dim(root_coupling, gx_index // BRANCH, 0, keepdims=False)
    root_field = jnp.einsum(
        "sik,skr->ir", root_row, root_coeffs, preferred_element_type=wide
    ).astype(narrow)
    top_picked = jnp.take(top_block, group_far[0], axis=0)
    top_field = (
        jnp.einsum("fik,fkr->ir", group_coupling[0], top_picked, preferred_element_type=wide)
        + jnp.dot(group_down[0], root_field, preferred_element_type=wide)
    ).astype(narrow)
    mid_block = mid_picked.reshape(-1, coeff_order, columns)
    mid_field = (
        jnp.einsum("fik,fkr->ir", cluster_coupling[0], mid_block, preferred_element_type=wide)
        + jnp.dot(cluster_down[0], top_field, preferred_element_type=wide)
    ).astype(narrow)
    coeff_rim = padded(leaf_coeffs.reshape(leaves, flat), ((("gx", "gy"), 0),), leaves)
    picked = jnp.take(coeff_rim, leaf_far - (first_leaf - leaves), axis=0).reshape(
        leaves, -1, coeff_order, columns
    )
    live_mask = (lax.broadcasted_iota(jnp.int32, leaf_far.shape, 1) < leaf_count[:, None]).astype(
        narrow
    )
    picked = picked * live_mask[:, :, None, None]
    leaf_field = (
        jnp.einsum("lfik,lfkr->lir", leaf_coupling, picked, preferred_element_type=wide)
        + jnp.einsum("lik,kr->lir", leaf_down, mid_field, preferred_element_type=wide)
    ).astype(narrow)
    far_part = jnp.einsum("lkr,lkm->lrm", leaf_field, basis_out, preferred_element_type=wide)
    values_rim = padded(densities, ((("gx", "gy"), 0),), REACH)
    shape_rim = padded(geometry, ((("gx", "gy"), 0),), REACH)
    near_local = near_ids - (first_leaf - REACH)

    def near_block(pieces):
        target, indices = pieces
        source = jnp.take(shape_rim, indices, axis=0)
        values = jnp.take(values_rim, indices, axis=0)
        kernel = near_kernel(target, source).astype(narrow)
        return jnp.einsum("bmnj,bnrj->brm", kernel, values, preferred_element_type=wide)

    near_part = lax.map(
        near_block,
        (
            geometry.reshape(leaves // leaf_block, leaf_block, 7, -1),
            near_local.reshape(leaves // leaf_block, leaf_block, -1),
        ),
    )
    return far_part + near_part.reshape(far_part.shape)


def solution(mesh):
    return jax.shard_map(
        on_device,
        mesh=mesh,
        in_specs=(
            P(("gx", "gy"), None, None),
            P(("gx", "gy"), None, None),
            P(("gx", "gy"), None),
            P(("gx", "gy"), None, None),
            P(("gx", "gy"), None, None),
            P(("gx", "gy"), None, None),
            P(("gx", "gy"), None, None),
            P(("gx", "gy"), None, None, None),
            P(("gx", "gy"), None),
            P(("gx", "gy")),
            P(("gx", "gy"), None, None),
            P(("gx", "gy"), None, None),
            P(("gx", "gy"), None, None, None),
            P(("gx", "gy"), None),
            P(),
            P("gx", None, None),
            P("gx", None, None, None),
            P("gx", None),
            P(),
        ),
        out_specs=P(("gx", "gy"), None, None),
        check_vma=False,
    )
```

profile of v0, /device:TPU:8, one launch (start us, length us, event | category | flops | bytes accessed | tf_op | source)
XLA Modules:
  0.0 328.0 jit_solution(2928487035204301218)
XLA Ops:
  0.0 2.6 convolution_convert_fusion
  4.9 9.3 %collective-permute-start.1 = (bf16[96,2048]{1,0:T(8,128)(2,1)}, bf16[96,2048]{1,0:T(8,128)(2,1)}, u32[]{:S(2)}, u32[]{:S(2)}) collective-permute-start(bf16[96,2048]{1,0:T(8,128)(2,1)} %copy.66), channel_id=1, source_target_pairs={{1,0},{2,1},{3,2},{4,3},{5,4},{6,5},{7,6},{8,7},{9,8},{10,9},{11,1... | collective-permute-start | bytes 1179656 | tf_op jit(solution)/shard_map/ppermute | solution.py:23
  14.2 1.9 collective-permute-start
  17.4 1.9 collective-permute-start.6
  19.3 8.0 %collective-permute-start.7 = (f32[4,7,128]{2,1,0:T(8,128)S(1)}, f32[4,7,128]{2,1,0:T(8,128)S(1)}, u32[]{:S(2)}, u32[]{:S(2)}) collective-permute-start(f32[4,7,128]{2,1,0:T(8,128)S(1)} %get-tuple-element.83), channel_id=1, source_target_pairs={{1,0},{2,1},{3,2},{4,3},{5,4},{6,5},{7,6},{8,7},{9,8},{10,9},{11,1... | collective-permute-start | bytes 43016 | tf_op jit(solution)/shard_map/ppermute | solution.py:23
  27.3 4.0 %copy.72 = bf16[96,64,64]{2,1,0:T(8,128)(2,1)} copy(bf16[96,64,64]{0,2,1:T(8,128)(2,1)} %param.26) | data formatting | bytes 1572864 | tf_op args[5]
  31.4 2.0 fusion.35
  33.5 12.8 %all-gather = bf16[8,1,2048]{2,1,0:T(2,128)(2,1)S(1)} all-gather(bf16[1,1,2048]{2,1,0:T(2,128)(2,1)S(1)} %reshape.240), channel_id=1, replica_groups=mesh['gx'=32,'gy'=8] {'gy'}, dimensions={0}, use_global_device_ids=true | all-gather | bytes 36864 | tf_op jit(solution)/shard_map/all_gather | solution.py:85
  50.4 24.5 %psum.7 = bf16[1,2048]{1,0:T(2,128)(2,1)S(1)} all-reduce(f32[1,2048]{1,0:T(1,128)S(1)} %reshape.189), channel_id=1, replica_groups=mesh['gx'=32,'gy'=8] {'gy'}, use_global_device_ids=true, to_apply=%region_0.0 | all-reduce | flops 2048 | bytes 12288 | tf_op jit(solution)/shard_map/psum | solution.py:86
  74.9 48.0 %all-gather.1 = bf16[32,1,2048]{2,1,0:T(2,128)(2,1)S(1)} all-gather(bf16[1,1,2048]{2,1,0:T(2,128)(2,1)S(1)} %bitcast.169), channel_id=1, replica_groups=mesh['gx'=32,'gy'=8] {'gx'}, dimensions={0}, use_global_device_ids=true | all-gather | bytes 135168 | tf_op jit(solution)/shard_map/all_gather | solution.py:89
  129.4 4.0 %copy.78 = bf16[96,64,64]{2,1,0:T(8,128)(2,1)} copy(bf16[96,64,64]{0,2,1:T(8,128)(2,1)} %param.27) | data formatting | bytes 1572864 | tf_op args[6]
  133.4 16.1 %copy.71 = bf16[96,6,64,64]{3,2,1,0:T(8,128)(2,1)} copy(bf16[96,6,64,64]{0,3,2,1:T(8,128)(2,1)} %param.28) | data formatting | bytes 9437184 | tf_op args[7]
  149.5 2.4 collective-permute-start.2
  152.0 1.9 collective-permute-start.4
  154.0 8.0 %collective-permute-start.5 = (bf16[4,32,128]{2,1,0:T(8,128)(2,1)S(1)}, bf16[4,32,128]{2,1,0:T(8,128)(2,1)S(1)}, u32[]{:S(2)}, u32[]{:S(2)}) collective-permute-start(bf16[4,32,128]{2,1,0:T(8,128)(2,1)S(1)} %get-tuple-element.81), channel_id=1, source_target_pairs={{1,0},{2,1},{3,2},{4,3},{5,4},{6,5},{7,6},{8,7},{9,8},{10,9},{11,1... | collective-permute-start | bytes 98312 | tf_op jit(solution)/shard_map/ppermute | solution.py:23
  164.7 130.7 %while.10 = (s32[]{:T(128)}, f32[12,8,32,128]{3,2,1,0:T(8,128)}, s32[12,8,8]{2,1,0:T(8,128)}, bf16[104,32,128]{2,1,0:T(8,128)(2,1)S(1)}, f32[104,7,128]{2,1,0:T(...) while((s32[]{:T(128)}, f32[12,8,32,128]{3,2,1,0:T(8,128)}, s32[12,8,8]{2,1,0:T(8,128)}, ...), condition=%wide.region_3.4_spmd, body=%wide.region_2.3_spmd.sunk | while | flops 87352896 | bytes 3410213 | solution.py:133
  169.7 5.9 %fusion.84 = f32[12,8,32,128]{3,2,1,0:T(8,128)} fusion(f32[12,8,32,128]{3,2,1,0:T(8,128)} %get-tuple-element.149, s32[]{:T(128)S(6)} %copy.97, f32[8,8,128]{2,1,0:T(8,128)S(1)} %bitcast.159, f32[8,128]{1,0:T(8,128)} %get-tuple-element.132, f32[8,8,128]{2,1,0:T(8,128)S(1)} %bitcast.160, f32[8,8,128]{2,1,0:T(8,128)S(1)} %bitcast.161, ...), kind=kOutput, calls=%fused_computation.21.clone.1 | convolution fusion | flops 87293952 | bytes 897092 | tf_op jit(solution)/shard_map/while/body/eval_jaxpr/bmnj,bnrj->brm/dot_general | solution.py:131
  180.6 5.9 %fusion.84 = f32[12,8,32,128]{3,2,1,0:T(8,128)} fusion(f32[12,8,32,128]{3,2,1,0:T(8,128)} %get-tuple-element.149, s32[]{:T(128)S(6)} %copy.97, f32[8,8,128]{2,1,0:T(8,128)S(1)} %bitcast.159, f32[8,128]{1,0:T(8,128)} %get-tuple-element.132, f32[8,8,128]{2,1,0:T(8,128)S(1)} %bitcast.160, f32[8,8,128]{2,1,0:T(8,128)S(1)} %bitcast.161, ...), kind=kOutput, calls=%fused_computation.21.clone.1 | convolution fusion | flops 87293952 | bytes 897092 | tf_op jit(solution)/shard_map/while/body/eval_jaxpr/bmnj,bnrj->brm/dot_general | solution.py:131
  191.5 5.9 %fusion.84 = f32[12,8,32,128]{3,2,1,0:T(8,128)} fusion(f32[12,8,32,128]{3,2,1,0:T(8,128)} %get-tuple-element.149, s32[]{:T(128)S(6)} %copy.97, f32[8,8,128]{2,1,0:T(8,128)S(1)} %bitcast.159, f32[8,128]{1,0:T(8,128)} %get-tuple-element.132, f32[8,8,128]{2,1,0:T(8,128)S(1)} %bitcast.160, f32[8,8,128]{2,1,0:T(8,128)S(1)} %bitcast.161, ...), kind=kOutput, calls=%fused_computation.21.clone.1 | convolution fusion | flops 87293952 | bytes 897092 | tf_op jit(solution)/shard_map/while/body/eval_jaxpr/bmnj,bnrj->brm/dot_general | solution.py:131
  202.4 5.9 %fusion.84 = f32[12,8,32,128]{3,2,1,0:T(8,128)} fusion(f32[12,8,32,128]{3,2,1,0:T(8,128)} %get-tuple-element.149, s32[]{:T(128)S(6)} %copy.97, f32[8,8,128]{2,1,0:T(8,128)S(1)} %bitcast.159, f32[8,128]{1,0:T(8,128)} %get-tuple-element.132, f32[8,8,128]{2,1,0:T(8,128)S(1)} %bitcast.160, f32[8,8,128]{2,1,0:T(8,128)S(1)} %bitcast.161, ...), kind=kOutput, calls=%fused_computation.21.clone.1 | convolution fusion | flops 87293952 | bytes 897092 | tf_op jit(solution)/shard_map/while/body/eval_jaxpr/bmnj,bnrj->brm/dot_general | solution.py:131
  213.3 5.9 %fusion.84 = f32[12,8,32,128]{3,2,1,0:T(8,128)} fusion(f32[12,8,32,128]{3,2,1,0:T(8,128)} %get-tuple-element.149, s32[]{:T(128)S(6)} %copy.97, f32[8,8,128]{2,1,0:T(8,128)S(1)} %bitcast.159, f32[8,128]{1,0:T(8,128)} %get-tuple-element.132, f32[8,8,128]{2,1,0:T(8,128)S(1)} %bitcast.160, f32[8,8,128]{2,1,0:T(8,128)S(1)} %bitcast.161, ...), kind=kOutput, calls=%fused_computation.21.clone.1 | convolution fusion | flops 87293952 | bytes 897092 | tf_op jit(solution)/shard_map/while/body/eval_jaxpr/bmnj,bnrj->brm/dot_general | solution.py:131
  224.2 5.9 %fusion.84 = f32[12,8,32,128]{3,2,1,0:T(8,128)} fusion(f32[12,8,32,128]{3,2,1,0:T(8,128)} %get-tuple-element.149, s32[]{:T(128)S(6)} %copy.97, f32[8,8,128]{2,1,0:T(8,128)S(1)} %bitcast.159, f32[8,128]{1,0:T(8,128)} %get-tuple-element.132, f32[8,8,128]{2,1,0:T(8,128)S(1)} %bitcast.160, f32[8,8,128]{2,1,0:T(8,128)S(1)} %bitcast.161, ...), kind=kOutput, calls=%fused_computation.21.clone.1 | convolution fusion | flops 87293952 | bytes 897092 | tf_op jit(solution)/shard_map/while/body/eval_jaxpr/bmnj,bnrj->brm/dot_general | solution.py:131
  235.1 5.9 %fusion.84 = f32[12,8,32,128]{3,2,1,0:T(8,128)} fusion(f32[12,8,32,128]{3,2,1,0:T(8,128)} %get-tuple-element.149, s32[]{:T(128)S(6)} %copy.97, f32[8,8,128]{2,1,0:T(8,128)S(1)} %bitcast.159, f32[8,128]{1,0:T(8,128)} %get-tuple-element.132, f32[8,8,128]{2,1,0:T(8,128)S(1)} %bitcast.160, f32[8,8,128]{2,1,0:T(8,128)S(1)} %bitcast.161, ...), kind=kOutput, calls=%fused_computation.21.clone.1 | convolution fusion | flops 87293952 | bytes 897092 | tf_op jit(solution)/shard_map/while/body/eval_jaxpr/bmnj,bnrj->brm/dot_general | solution.py:131
  246.0 5.9 %fusion.84 = f32[12,8,32,128]{3,2,1,0:T(8,128)} fusion(f32[12,8,32,128]{3,2,1,0:T(8,128)} %get-tuple-element.149, s32[]{:T(128)S(6)} %copy.97, f32[8,8,128]{2,1,0:T(8,128)S(1)} %bitcast.159, f32[8,128]{1,0:T(8,128)} %get-tuple-element.132, f32[8,8,128]{2,1,0:T(8,128)S(1)} %bitcast.160, f32[8,8,128]{2,1,0:T(8,128)S(1)} %bitcast.161, ...), kind=kOutput, calls=%fused_computation.21.clone.1 | convolution fusion | flops 87293952 | bytes 897092 | tf_op jit(solution)/shard_map/while/body/eval_jaxpr/bmnj,bnrj->brm/dot_general | solution.py:131
  256.9 5.9 %fusion.84 = f32[12,8,32,128]{3,2,1,0:T(8,128)} fusion(f32[12,8,32,128]{3,2,1,0:T(8,128)} %get-tuple-element.149, s32[]{:T(128)S(6)} %copy.97, f32[8,8,128]{2,1,0:T(8,128)S(1)} %bitcast.159, f32[8,128]{1,0:T(8,128)} %get-tuple-element.132, f32[8,8,128]{2,1,0:T(8,128)S(1)} %bitcast.160, f32[8,8,128]{2,1,0:T(8,128)S(1)} %bitcast.161, ...), kind=kOutput, calls=%fused_computation.21.clone.1 | convolution fusion | flops 87293952 | bytes 897092 | tf_op jit(solution)/shard_map/while/body/eval_jaxpr/bmnj,bnrj->brm/dot_general | solution.py:131
  267.8 5.9 %fusion.84 = f32[12,8,32,128]{3,2,1,0:T(8,128)} fusion(f32[12,8,32,128]{3,2,1,0:T(8,128)} %get-tuple-element.149, s32[]{:T(128)S(6)} %copy.97, f32[8,8,128]{2,1,0:T(8,128)S(1)} %bitcast.159, f32[8,128]{1,0:T(8,128)} %get-tuple-element.132, f32[8,8,128]{2,1,0:T(8,128)S(1)} %bitcast.160, f32[8,8,128]{2,1,0:T(8,128)S(1)} %bitcast.161, ...), kind=kOutput, calls=%fused_computation.21.clone.1 | convolution fusion | flops 87293952 | bytes 897092 | tf_op jit(solution)/shard_map/while/body/eval_jaxpr/bmnj,bnrj->brm/dot_general | solution.py:131
  278.7 5.9 %fusion.84 = f32[12,8,32,128]{3,2,1,0:T(8,128)} fusion(f32[12,8,32,128]{3,2,1,0:T(8,128)} %get-tuple-element.149, s32[]{:T(128)S(6)} %copy.97, f32[8,8,128]{2,1,0:T(8,128)S(1)} %bitcast.159, f32[8,128]{1,0:T(8,128)} %get-tuple-element.132, f32[8,8,128]{2,1,0:T(8,128)S(1)} %bitcast.160, f32[8,8,128]{2,1,0:T(8,128)S(1)} %bitcast.161, ...), kind=kOutput, calls=%fused_computation.21.clone.1 | convolution fusion | flops 87293952 | bytes 897092 | tf_op jit(solution)/shard_map/while/body/eval_jaxpr/bmnj,bnrj->brm/dot_general | solution.py:131
  289.6 5.9 %fusion.84 = f32[12,8,32,128]{3,2,1,0:T(8,128)} fusion(f32[12,8,32,128]{3,2,1,0:T(8,128)} %get-tuple-element.149, s32[]{:T(128)S(6)} %copy.97, f32[8,8,128]{2,1,0:T(8,128)S(1)} %bitcast.159, f32[8,128]{1,0:T(8,128)} %get-tuple-element.132, f32[8,8,128]{2,1,0:T(8,128)S(1)} %bitcast.160, f32[8,8,128]{2,1,0:T(8,128)S(1)} %bitcast.161, ...), kind=kOutput, calls=%fused_computation.21.clone.1 | convolution fusion | flops 87293952 | bytes 897092 | tf_op jit(solution)/shard_map/while/body/eval_jaxpr/bmnj,bnrj->brm/dot_general | solution.py:131
  296.5 4.3 %fusion.37 = f32[32,96,64]{2,0,1:T(8,128)} fusion(bf16[96,64,64]{2,1,0:T(8,128)(2,1)} %copy.78, f32[32,64]{1,0:T(8,128)S(1)} %convolution_bitcast_fusion.3, bf16[32,64]{1,0:T(8,128)(2,1)} %fusion.33, bf16[1,64,64]{2,1,0:T(8,128)(2,1)} %param.32), kind=kOutput, calls=%fused_computation.60 | convolution fusion | flops 25432064 | bytes 1593344 | tf_op jit(solution)/shard_map/lik,kr->lir/dot_general | solution.py:119
  302.1 4.0 %gather_fusion.2 = bf16[576,2048]{1,0:T(8,128)(2,1)} fusion(bf16[288,2048]{1,0:T(8,128)(2,1)S(1)} %pad_maximum_fusion, s32[1024]{0:T(1024)S(1)} %pad_clamp_fusion.3), kind=kCustom, calls=%fused_computation.2 | custom fusion | bytes 4720896 | tf_op jit(solution)/shard_map/jit(_take)/gather | solution.py:110
  306.1 11.7 %gather.23 = bf16[96,6,64,32]{3,2,1,0:T(8,128)(2,1)} reshape(bf16[576,2048]{1,0:T(8,128)(2,1)} %gather_fusion.2) | data formatting | bytes 4718592 | tf_op jit(solution)/shard_map/jit(_take)/gather | solution.py:110
  317.8 10.3 %bitcast_add_fusion.1 = f32[96,32,128]{2,1,0:T(8,128)} fusion(f32[12,8,32,128]{3,2,1,0:T(8,128)} %get-tuple-element.37, bf16[96,64,128]{2,1,0:T(8,128)(2,1)S(1)} %copy-done, f32[32,96,64]{2,0,1:T(8,128)S(1)} %copy-done.1, bf16[96,6,64,64]{3,2,1,0:T(8,128)(2,1)} %copy.71, bf16[96,6,64,32]{3,2,1,0:T(8,128)(2,1)} %gather.23, pred[96,6]{1,0:T(8,128)(4,1)S(1)} %copy-done.6, ...), kind=kOutput, calls=%fused_computation.44 | convolution fusion | flops 204472320 | bytes 12584640 | tf_op jit(solution)/shard_map/lkr,lkm->lrm/dot_general | solution.py:121
  (193 shorter events, 79.2 us)
Async XLA Ops:
  0.0 317.8 %copy-start = (bf16[96,64,128]{2,1,0:T(8,128)(2,1)S(1)}, bf16[96,64,128]{2,1,0:T(8,128)(2,1)}, u32[]{:S(2)}) copy-start(bf16[96,64,128]{2,1,0:T(8,128)(2,1)} %param.25) | copy-start | bytes 4718596
  4.9 295.9 %collective-permute-start.1 = (bf16[96,2048]{1,0:T(8,128)(2,1)}, bf16[96,2048]{1,0:T(8,128)(2,1)}, u32[]{:S(2)}, u32[]{:S(2)}) collective-permute-start(bf16[96,2048]{1,0:T(8,128)(2,1)} %copy.66), channel_id=1, source_target_pairs={{1,0},{2,1},{3,2},{4,3},{5,4},{6,5},{7,6},{8,7},{9,8},{10,9},{11,1... | collective-permute-start | bytes 1179656 | tf_op jit(solution)/shard_map/ppermute | solution.py:23
  14.2 286.6 %collective-permute-start = (bf16[96,2048]{1,0:T(8,128)(2,1)}, bf16[96,2048]{1,0:T(8,128)(2,1)}, u32[]{:S(2)}, u32[]{:S(2)}) collective-permute-start(bf16[96,2048]{1,0:T(8,128)(2,1)} %copy.66), channel_id=1, source_target_pairs={{0,1},{1,2},{2,3},{3,4},{4,5},{5,6},{6,7},{7,8},{8,9},{9,10},{10,1... | collective-permute-start | bytes 1179656 | tf_op jit(solution)/shard_map/ppermute | solution.py:21
  17.4 132.2 %collective-permute-start.6 = (f32[4,7,128]{2,1,0:T(8,128)S(1)}, f32[4,7,128]{2,1,0:T(8,128)S(1)}, u32[]{:S(2)}, u32[]{:S(2)}) collective-permute-start(f32[4,7,128]{2,1,0:T(8,128)S(1)} %get-tuple-element.82), channel_id=1, source_target_pairs={{0,1},{1,2},{2,3},{3,4},{4,5},{5,6},{6,7},{7,8},{8,9},{9,10},{10,1... | collective-permute-start | bytes 43016 | tf_op jit(solution)/shard_map/ppermute | solution.py:21
  19.3 29.0 %copy-start.10 = (s32[1,6]{1,0:T(1,128)S(1)}, s32[1,6]{1,0:T(1,128)}, u32[]{:S(2)}) copy-start(s32[1,6]{1,0:T(1,128)} %param.34) | copy-start | bytes 76
  19.3 29.0 %copy-start.11 = (s32[1,6]{1,0:T(1,128)S(1)}, s32[1,6]{1,0:T(1,128)}, u32[]{:S(2)}) copy-start(s32[1,6]{1,0:T(1,128)} %param.38) | copy-start | bytes 76
  19.3 29.8 %copy-start.9 = (s32[96]{0:T(128)S(1)}, s32[96]{0:T(128)}, u32[]{:S(2)}) copy-start(s32[96]{0:T(128)} %param.30) | copy-start | bytes 1156
  19.3 30.5 %copy-start.7 = (s32[96,6]{0,1:T(8,128)S(1)}, s32[96,6]{0,1:T(8,128)}, u32[]{:S(2)}) copy-start(s32[96,6]{0,1:T(8,128)} %param.29) | copy-start | bytes 6916
  19.3 30.8 %copy-start.4 = (bf16[1,64,64]{2,1,0:T(8,128)(2,1)S(1)}, bf16[1,64,64]{2,1,0:T(8,128)(2,1)}, u32[]{:S(2)}) copy-start(bf16[1,64,64]{2,1,0:T(8,128)(2,1)} %param.31) | copy-start | bytes 24580
  19.3 132.6 %collective-permute-start.7 = (f32[4,7,128]{2,1,0:T(8,128)S(1)}, f32[4,7,128]{2,1,0:T(8,128)S(1)}, u32[]{:S(2)}, u32[]{:S(2)}) collective-permute-start(f32[4,7,128]{2,1,0:T(8,128)S(1)} %get-tuple-element.83), channel_id=1, source_target_pairs={{1,0},{2,1},{3,2},{4,3},{5,4},{6,5},{7,6},{8,7},{9,8},{10,9},{11,1... | collective-permute-start | bytes 43016 | tf_op jit(solution)/shard_map/ppermute | solution.py:23
  31.4 92.7 %copy-start.2 = (bf16[32,64,64]{2,1,0:T(8,128)(2,1)S(1)}, bf16[32,64,64]{2,1,0:T(8,128)(2,1)}, u32[]{:S(2)}) copy-start(bf16[32,64,64]{2,1,0:T(8,128)(2,1)} %param.35) | copy-start | bytes 786436
  31.4 93.7 %copy-start.8 = (s32[96,8]{0,1:T(8,128)S(1)}, s32[96,8]{0,1:T(8,128)}, u32[]{:S(2)}) copy-start(s32[96,8]{0,1:T(8,128)} %param.23) | copy-start | bytes 9220
  33.3 92.9 %copy-start.5 = (bf16[1,64,64]{2,1,0:T(8,128)(2,1)S(1)}, bf16[1,64,64]{2,1,0:T(8,128)(2,1)}, u32[]{:S(2)}) copy-start(bf16[1,64,64]{2,1,0:T(8,128)(2,1)} %param.36) | copy-start | bytes 24580
  46.3 107.6 %collective-permute-start.3 = (bf16[8,2048]{1,0:T(8,128)(2,1)S(1)}, bf16[8,2048]{1,0:T(8,128)(2,1)S(1)}, u32[]{:S(2)}, u32[]{:S(2)}) collective-permute-start(bf16[8,2048]{1,0:T(8,128)(2,1)S(1)} %bitcast.165), channel_id=1, source_target_pairs={{8,0},{16,8},{24,16},{32,24},{40,32},{48,40},{56,48},{64,56},{72,6... | collective-permute-start | bytes 98312 | tf_op jit(solution)/shard_map/ppermute | solution.py:23
  149.5 12.5 %collective-permute-start.2 = (bf16[8,2048]{1,0:T(8,128)(2,1)S(1)}, bf16[8,2048]{1,0:T(8,128)(2,1)S(1)}, u32[]{:S(2)}, u32[]{:S(2)}) collective-permute-start(bf16[8,2048]{1,0:T(8,128)(2,1)S(1)} %bitcast.166), channel_id=1, source_target_pairs={{0,8},{8,16},{16,24},{24,32},{32,40},{40,48},{48,56},{56,64},{64,7... | collective-permute-start | bytes 98312 | tf_op jit(solution)/shard_map/ppermute | solution.py:21
  152.0 11.5 %collective-permute-start.4 = (bf16[4,32,128]{2,1,0:T(8,128)(2,1)S(1)}, bf16[4,32,128]{2,1,0:T(8,128)(2,1)S(1)}, u32[]{:S(2)}, u32[]{:S(2)}) collective-permute-start(bf16[4,32,128]{2,1,0:T(8,128)(2,1)S(1)} %get-tuple-element.80), channel_id=1, source_target_pairs={{0,1},{1,2},{2,3},{3,4},{4,5},{5,6},{6,7},{7,8},{8,9},{9,10},{10,1... | collective-permute-start | bytes 98312 | tf_op jit(solution)/shard_map/ppermute | solution.py:21
  154.0 9.5 %collective-permute-start.5 = (bf16[4,32,128]{2,1,0:T(8,128)(2,1)S(1)}, bf16[4,32,128]{2,1,0:T(8,128)(2,1)S(1)}, u32[]{:S(2)}, u32[]{:S(2)}) collective-permute-start(bf16[4,32,128]{2,1,0:T(8,128)(2,1)S(1)} %get-tuple-element.81), channel_id=1, source_target_pairs={{1,0},{2,1},{3,2},{4,3},{5,4},{6,5},{7,6},{8,7},{9,8},{10,9},{11,1... | collective-permute-start | bytes 98312 | tf_op jit(solution)/shard_map/ppermute | solution.py:23
  306.1 11.7 %copy-start.1 = (f32[32,96,64]{2,0,1:T(8,128)S(1)}, f32[32,96,64]{2,0,1:T(8,128)}, u32[]{:S(2)}) copy-start(f32[32,96,64]{2,0,1:T(8,128)} %fusion.37) | copy-start | bytes 2359300
  306.1 11.7 %copy-start.3 = (bf16[96,6]{1,0:T(8,128)(2,1)S(1)}, bf16[96,6]{1,0:T(8,128)(2,1)}, u32[]{:S(2)}) copy-start(bf16[96,6]{1,0:T(8,128)(2,1)} %fusion.49) | copy-start | bytes 3460
  306.1 11.7 %copy-start.6 = (pred[96,6]{1,0:T(8,128)(4,1)S(1)}, pred[96,6]{1,0:T(8,128)(4,1)}, u32[]{:S(2)}) copy-start(pred[96,6]{1,0:T(8,128)(4,1)} %copy.64) | copy-start | bytes 1732
where the time goes:
time: 331 us; the launch traced here: 328 us
  matrix products  94.2 us (28%)
  local copies, waits for them, and re-layouts  90.2 us (27%)
  blocking collectives  85.2 us (26%)
  starting transfers between devices  35.4 us (11%)
  other arithmetic  22.2 us (7%)
    dot_general x12, matrix products, near_block(): jnp.einsum('bmnj,bnrj->brm', kernel, values, preferred_element_type=wide)  70.5 us
    all_gather x1, blocking collectives, on_device(): lax.all_gather(group_sum.astype(narrow), 'gx', axis=0, tiled=True)  48 us
    ppermute x4, starting transfers between devices, padded(): lax.ppermute(head, axis, [((i + 1) % count, i) for i in range(ends)])  27.2 us
    unnamed x30, local copies, waits for them, and re-layouts  25.5 us
    psum x1, blocking collectives, on_device(): group_sum = lax.psum(mid_term, 'gy')  24.5 us
    gather x2, local copies, waits for them, and re-layouts, on_device(): jnp.take(coeff_rim, leaf_far - (first_leaf - leaves), axis=0)  15.6 us
    all_gather x1, blocking collectives, on_device(): siblings = lax.all_gather(mid_flat, 'gy', axis=0, tiled=True)  12.8 us
    dot_general x1, matrix products, on_device(): jnp.einsum('lkr,lkm->lrm', leaf_field, basis_out, preferred_element_type=...  10.3 us
  transfers between devices with their start and end apart: 8, of which 0 were waited for; matrix products, arithmetic and copies ran while one was open for 53% of the time, Pallas kernels for 0%

commit v1 on v0

--- a/solution.py
+++ b/solution.py
@@ -86,7 +86,10 @@
     group_sum = lax.psum(mid_term, "gy")
     nearby = padded(siblings, (("gx", 0),), group_size)
     mid_picked = jnp.take(nearby, cluster_far[0] - (gx_index - 1) * group_size, axis=0)
-    top_coeffs = lax.all_gather(group_sum.astype(narrow), "gx", axis=0, tiled=True)
+    top_coeffs = jnp.concatenate(
+        lax.all_to_all(jnp.stack([group_sum.astype(narrow)] * lax.axis_size("gx")), "gx", 0, 0),
+        axis=0,
+    )
     top_block = top_coeffs.reshape(groups, coeff_order, columns)
     root_terms = jnp.einsum("gik,gkr->gir", group_up, top_block, preferred_element_type=wide)
     root_coeffs = jnp.sum(

time: 331 us -> 296 us (0.89)
  blocking collectives: 85.2 us -> 36.7 us
  other arithmetic: 22.2 us -> 27.5 us
  local copies, waits for them, and re-layouts: 90.2 us -> 95 us
    all_gather x1 -> x0, blocking collectives: 48 us -> none  [on_device(): lax.all_gather(group_sum.astype(narrow), 'gx', axis=0, tiled=True)]
    all_to_all x0 -> x1, starting transfers between devices: none -> 5.65 us  [on_device(): lax.all_to_all(jnp.stack([group_sum.astype(narrow)] * lax.axis_size('gx')...]
    unnamed x30 -> x36, local copies, waits for them, and re-layouts: 25.5 us -> 28.2 us
  transfers between devices with their start and end apart: 8 -> 9, of which waited for: 0 -> 0; matrix products, arithmetic and copies ran while one was open for 53% -> 63% of each run, Pallas kernels for 0% -> 0%
where the time goes in v1:
time: 296 us; the launch traced here: 292 us
  local copies, waits for them, and re-layouts  95 us (32%)
  matrix products  94 us (32%)
  starting transfers between devices  38.5 us (13%)
  blocking collectives  36.7 us (12%)
  other arithmetic  27.5 us (9%)
    dot_general x12, matrix products, near_block(): jnp.einsum('bmnj,bnrj->brm', kernel, values, preferred_element_type=wide)  70.5 us
    unnamed x36, local copies, waits for them, and re-layouts  28.2 us
    ppermute x4, starting transfers between devices, padded(): lax.ppermute(head, axis, [((i + 1) % count, i) for i in range(ends)])  24.5 us
    psum x1, blocking collectives, on_device(): group_sum = lax.psum(mid_term, 'gy')  23.9 us
    gather x2, local copies, waits for them, and re-layouts, on_device(): jnp.take(coeff_rim, leaf_far - (first_leaf - leaves), axis=0)  15.6 us
    all_gather x1, blocking collectives, on_device(): siblings = lax.all_gather(mid_flat, 'gy', axis=0, tiled=True)  12.8 us
    dot_general x1, matrix products, on_device(): jnp.einsum('lkr,lkm->lrm', leaf_field, basis_out, preferred_element_type=...  10.3 us
    slice x12, local copies, waits for them, and re-layouts, near_kernel(): panel_area = source[:, None, :, 6, :]  9.31 us
  transfers between devices with their start and end apart: 9, of which 0 were waited for; matrix products, arithmetic and copies ran while one was open for 63% of the time, Pallas kernels for 0%

profile of v1, /device:TPU:8, one launch (start us, length us, event | category | flops | bytes accessed | tf_op | source)
XLA Modules:
  0.0 292.4 jit_solution(941053071900236881)
XLA Ops:
  0.0 2.6 convolution_convert_fusion
  4.9 9.3 %collective-permute-start.1 = (bf16[96,2048]{1,0:T(8,128)(2,1)}, bf16[96,2048]{1,0:T(8,128)(2,1)}, u32[]{:S(2)}, u32[]{:S(2)}) collective-permute-start(bf16[96,2048]{1,0:T(8,128)(2,1)} %copy.66), channel_id=1, source_target_pairs={{1,0},{2,1},{3,2},{4,3},{5,4},{6,5},{7,6},{8,7},{9,8},{10,9},{11,1... | collective-permute-start | bytes 1179656 | tf_op jit(solution)/shard_map/ppermute | solution.py:23
  14.2 1.9 collective-permute-start
  20.0 1.9 collective-permute-start.6
  22.0 7.9 %collective-permute-start.7 = (f32[4,7,128]{2,1,0:T(8,128)S(1)}, f32[4,7,128]{2,1,0:T(8,128)S(1)}, u32[]{:S(2)}, u32[]{:S(2)}) collective-permute-start(f32[4,7,128]{2,1,0:T(8,128)S(1)} %get-tuple-element.83), channel_id=1, source_target_pairs={{1,0},{2,1},{3,2},{4,3},{5,4},{6,5},{7,6},{8,7},{9,8},{10,9},{11,1... | collective-permute-start | bytes 43016 | tf_op jit(solution)/shard_map/ppermute | solution.py:23
  29.8 4.0 %copy.72 = bf16[96,64,64]{2,1,0:T(8,128)(2,1)} copy(bf16[96,64,64]{0,2,1:T(8,128)(2,1)} %param.26) | data formatting | bytes 1572864 | tf_op args[5]
  33.9 2.0 fusion.35
  36.2 23.9 %psum.7 = bf16[1,2048]{1,0:T(2,128)(2,1)S(1)} all-reduce(f32[1,2048]{1,0:T(1,128)S(1)} %reshape.189), channel_id=1, replica_groups=mesh['gx'=32,'gy'=8] {'gy'}, use_global_device_ids=true, to_apply=%region_0.0 | all-reduce | flops 2048 | bytes 12288 | tf_op jit(solution)/shard_map/psum | solution.py:86
  62.9 5.6 %all-to-all-start = ((bf16[32,2,1024]{2,1,0:T(2,128)(2,1)}), bf16[32,2,1024]{2,1,0:T(2,128)(2,1)}, u32[]{:S(2)}, u32[]{:S(2)}) async-start(bf16[32,2,1024]{2,1,0:T(2,128)(2,1)} %reshape.251), calls=%async_computation | async-start | bytes 262144 | tf_op jit(solution)/shard_map/all_to_all | solution.py:90
  73.6 12.8 %all-gather = bf16[8,1,2048]{2,1,0:T(2,128)(2,1)S(1)} all-gather(bf16[1,1,2048]{2,1,0:T(2,128)(2,1)S(1)} %reshape.239), channel_id=1, replica_groups=mesh['gx'=32,'gy'=8] {'gy'}, dimensions={0}, use_global_device_ids=true | all-gather | bytes 36864 | tf_op jit(solution)/shard_map/all_gather | solution.py:85
  86.9 4.0 %copy.78 = bf16[96,64,64]{2,1,0:T(8,128)(2,1)} copy(bf16[96,64,64]{0,2,1:T(8,128)(2,1)} %param.27) | data formatting | bytes 1572864 | tf_op args[6]
  90.9 16.1 %copy.71 = bf16[96,6,64,64]{3,2,1,0:T(8,128)(2,1)} copy(bf16[96,6,64,64]{0,3,2,1:T(8,128)(2,1)} %param.28) | data formatting | bytes 9437184 | tf_op args[7]
  107.0 4.0 %collective-permute-start.5 = (bf16[4,32,128]{2,1,0:T(8,128)(2,1)S(1)}, bf16[4,32,128]{2,1,0:T(8,128)(2,1)S(1)}, u32[]{:S(2)}, u32[]{:S(2)}) collective-permute-start(bf16[4,32,128]{2,1,0:T(8,128)(2,1)S(1)} %get-tuple-element.81), channel_id=1, source_target_pairs={{1,0},{2,1},{3,2},{4,3},{5,4},{6,5},{7,6},{8,7},{9,8},{10,9},{11,1... | collective-permute-start | bytes 98312 | tf_op jit(solution)/shard_map/ppermute | solution.py:23
  111.0 3.4 %collective-permute-start.3 = (bf16[8,2048]{1,0:T(8,128)(2,1)}, bf16[8,2048]{1,0:T(8,128)(2,1)}, u32[]{:S(2)}, u32[]{:S(2)}) collective-permute-start(bf16[8,2048]{1,0:T(8,128)(2,1)} %bitcast.123), channel_id=1, source_target_pairs={{8,0},{16,8},{24,16},{32,24},{40,32},{48,40},{56,48},{64,56},{72,6... | collective-permute-start | bytes 98312 | tf_op jit(solution)/shard_map/ppermute | solution.py:23
  114.4 2.7 collective-permute-start.2
  118.4 130.7 %while.10 = (s32[]{:T(128)}, f32[12,8,32,128]{3,2,1,0:T(8,128)}, s32[12,8,8]{2,1,0:T(8,128)}, bf16[104,32,128]{2,1,0:T(8,128)(2,1)S(1)}, f32[104,7,128]{2,1,0:T(...) while((s32[]{:T(128)}, f32[12,8,32,128]{3,2,1,0:T(8,128)}, s32[12,8,8]{2,1,0:T(8,128)}, ...), condition=%wide.region_3.4_spmd, body=%wide.region_2.3_spmd.sunk | while | flops 87352896 | bytes 3410213 | solution.py:136
  123.4 5.9 %fusion.84 = f32[12,8,32,128]{3,2,1,0:T(8,128)} fusion(f32[12,8,32,128]{3,2,1,0:T(8,128)} %get-tuple-element.149, s32[]{:T(128)S(6)} %copy.97, f32[8,8,128]{2,1,0:T(8,128)S(1)} %bitcast.156, f32[8,128]{1,0:T(8,128)} %get-tuple-element.132, f32[8,8,128]{2,1,0:T(8,128)S(1)} %bitcast.157, f32[8,8,128]{2,1,0:T(8,128)S(1)} %bitcast.158, ...), kind=kOutput, calls=%fused_computation.21.clone.1 | convolution fusion | flops 87293952 | bytes 897092 | tf_op jit(solution)/shard_map/while/body/eval_jaxpr/bmnj,bnrj->brm/dot_general | solution.py:134
  134.3 5.9 %fusion.84 = f32[12,8,32,128]{3,2,1,0:T(8,128)} fusion(f32[12,8,32,128]{3,2,1,0:T(8,128)} %get-tuple-element.149, s32[]{:T(128)S(6)} %copy.97, f32[8,8,128]{2,1,0:T(8,128)S(1)} %bitcast.156, f32[8,128]{1,0:T(8,128)} %get-tuple-element.132, f32[8,8,128]{2,1,0:T(8,128)S(1)} %bitcast.157, f32[8,8,128]{2,1,0:T(8,128)S(1)} %bitcast.158, ...), kind=kOutput, calls=%fused_computation.21.clone.1 | convolution fusion | flops 87293952 | bytes 897092 | tf_op jit(solution)/shard_map/while/body/eval_jaxpr/bmnj,bnrj->brm/dot_general | solution.py:134
  145.2 5.9 %fusion.84 = f32[12,8,32,128]{3,2,1,0:T(8,128)} fusion(f32[12,8,32,128]{3,2,1,0:T(8,128)} %get-tuple-element.149, s32[]{:T(128)S(6)} %copy.97, f32[8,8,128]{2,1,0:T(8,128)S(1)} %bitcast.156, f32[8,128]{1,0:T(8,128)} %get-tuple-element.132, f32[8,8,128]{2,1,0:T(8,128)S(1)} %bitcast.157, f32[8,8,128]{2,1,0:T(8,128)S(1)} %bitcast.158, ...), kind=kOutput, calls=%fused_computation.21.clone.1 | convolution fusion | flops 87293952 | bytes 897092 | tf_op jit(solution)/shard_map/while/body/eval_jaxpr/bmnj,bnrj->brm/dot_general | solution.py:134
  156.1 5.9 %fusion.84 = f32[12,8,32,128]{3,2,1,0:T(8,128)} fusion(f32[12,8,32,128]{3,2,1,0:T(8,128)} %get-tuple-element.149, s32[]{:T(128)S(6)} %copy.97, f32[8,8,128]{2,1,0:T(8,128)S(1)} %bitcast.156, f32[8,128]{1,0:T(8,128)} %get-tuple-element.132, f32[8,8,128]{2,1,0:T(8,128)S(1)} %bitcast.157, f32[8,8,128]{2,1,0:T(8,128)S(1)} %bitcast.158, ...), kind=kOutput, calls=%fused_computation.21.clone.1 | convolution fusion | flops 87293952 | bytes 897092 | tf_op jit(solution)/shard_map/while/body/eval_jaxpr/bmnj,bnrj->brm/dot_general | solution.py:134
  167.0 5.9 %fusion.84 = f32[12,8,32,128]{3,2,1,0:T(8,128)} fusion(f32[12,8,32,128]{3,2,1,0:T(8,128)} %get-tuple-element.149, s32[]{:T(128)S(6)} %copy.97, f32[8,8,128]{2,1,0:T(8,128)S(1)} %bitcast.156, f32[8,128]{1,0:T(8,128)} %get-tuple-element.132, f32[8,8,128]{2,1,0:T(8,128)S(1)} %bitcast.157, f32[8,8,128]{2,1,0:T(8,128)S(1)} %bitcast.158, ...), kind=kOutput, calls=%fused_computation.21.clone.1 | convolution fusion | flops 87293952 | bytes 897092 | tf_op jit(solution)/shard_map/while/body/eval_jaxpr/bmnj,bnrj->brm/dot_general | solution.py:134
  177.8 5.9 %fusion.84 = f32[12,8,32,128]{3,2,1,0:T(8,128)} fusion(f32[12,8,32,128]{3,2,1,0:T(8,128)} %get-tuple-element.149, s32[]{:T(128)S(6)} %copy.97, f32[8,8,128]{2,1,0:T(8,128)S(1)} %bitcast.156, f32[8,128]{1,0:T(8,128)} %get-tuple-element.132, f32[8,8,128]{2,1,0:T(8,128)S(1)} %bitcast.157, f32[8,8,128]{2,1,0:T(8,128)S(1)} %bitcast.158, ...), kind=kOutput, calls=%fused_computation.21.clone.1 | convolution fusion | flops 87293952 | bytes 897092 | tf_op jit(solution)/shard_map/while/body/eval_jaxpr/bmnj,bnrj->brm/dot_general | solution.py:134
  188.7 5.9 %fusion.84 = f32[12,8,32,128]{3,2,1,0:T(8,128)} fusion(f32[12,8,32,128]{3,2,1,0:T(8,128)} %get-tuple-element.149, s32[]{:T(128)S(6)} %copy.97, f32[8,8,128]{2,1,0:T(8,128)S(1)} %bitcast.156, f32[8,128]{1,0:T(8,128)} %get-tuple-element.132, f32[8,8,128]{2,1,0:T(8,128)S(1)} %bitcast.157, f32[8,8,128]{2,1,0:T(8,128)S(1)} %bitcast.158, ...), kind=kOutput, calls=%fused_computation.21.clone.1 | convolution fusion | flops 87293952 | bytes 897092 | tf_op jit(solution)/shard_map/while/body/eval_jaxpr/bmnj,bnrj->brm/dot_general | solution.py:134
  199.6 5.9 %fusion.84 = f32[12,8,32,128]{3,2,1,0:T(8,128)} fusion(f32[12,8,32,128]{3,2,1,0:T(8,128)} %get-tuple-element.149, s32[]{:T(128)S(6)} %copy.97, f32[8,8,128]{2,1,0:T(8,128)S(1)} %bitcast.156, f32[8,128]{1,0:T(8,128)} %get-tuple-element.132, f32[8,8,128]{2,1,0:T(8,128)S(1)} %bitcast.157, f32[8,8,128]{2,1,0:T(8,128)S(1)} %bitcast.158, ...), kind=kOutput, calls=%fused_computation.21.clone.1 | convolution fusion | flops 87293952 | bytes 897092 | tf_op jit(solution)/shard_map/while/body/eval_jaxpr/bmnj,bnrj->brm/dot_general | solution.py:134
  210.5 5.9 %fusion.84 = f32[12,8,32,128]{3,2,1,0:T(8,128)} fusion(f32[12,8,32,128]{3,2,1,0:T(8,128)} %get-tuple-element.149, s32[]{:T(128)S(6)} %copy.97, f32[8,8,128]{2,1,0:T(8,128)S(1)} %bitcast.156, f32[8,128]{1,0:T(8,128)} %get-tuple-element.132, f32[8,8,128]{2,1,0:T(8,128)S(1)} %bitcast.157, f32[8,8,128]{2,1,0:T(8,128)S(1)} %bitcast.158, ...), kind=kOutput, calls=%fused_computation.21.clone.1 | convolution fusion | flops 87293952 | bytes 897092 | tf_op jit(solution)/shard_map/while/body/eval_jaxpr/bmnj,bnrj->brm/dot_general | solution.py:134
  221.4 5.9 %fusion.84 = f32[12,8,32,128]{3,2,1,0:T(8,128)} fusion(f32[12,8,32,128]{3,2,1,0:T(8,128)} %get-tuple-element.149, s32[]{:T(128)S(6)} %copy.97, f32[8,8,128]{2,1,0:T(8,128)S(1)} %bitcast.156, f32[8,128]{1,0:T(8,128)} %get-tuple-element.132, f32[8,8,128]{2,1,0:T(8,128)S(1)} %bitcast.157, f32[8,8,128]{2,1,0:T(8,128)S(1)} %bitcast.158, ...), kind=kOutput, calls=%fused_computation.21.clone.1 | convolution fusion | flops 87293952 | bytes 897092 | tf_op jit(solution)/shard_map/while/body/eval_jaxpr/bmnj,bnrj->brm/dot_general | solution.py:134
  232.3 5.9 %fusion.84 = f32[12,8,32,128]{3,2,1,0:T(8,128)} fusion(f32[12,8,32,128]{3,2,1,0:T(8,128)} %get-tuple-element.149, s32[]{:T(128)S(6)} %copy.97, f32[8,8,128]{2,1,0:T(8,128)S(1)} %bitcast.156, f32[8,128]{1,0:T(8,128)} %get-tuple-element.132, f32[8,8,128]{2,1,0:T(8,128)S(1)} %bitcast.157, f32[8,8,128]{2,1,0:T(8,128)S(1)} %bitcast.158, ...), kind=kOutput, calls=%fused_computation.21.clone.1 | convolution fusion | flops 87293952 | bytes 897092 | tf_op jit(solution)/shard_map/while/body/eval_jaxpr/bmnj,bnrj->brm/dot_general | solution.py:134
  243.2 5.9 %fusion.84 = f32[12,8,32,128]{3,2,1,0:T(8,128)} fusion(f32[12,8,32,128]{3,2,1,0:T(8,128)} %get-tuple-element.149, s32[]{:T(128)S(6)} %copy.97, f32[8,8,128]{2,1,0:T(8,128)S(1)} %bitcast.156, f32[8,128]{1,0:T(8,128)} %get-tuple-element.132, f32[8,8,128]{2,1,0:T(8,128)S(1)} %bitcast.157, f32[8,8,128]{2,1,0:T(8,128)S(1)} %bitcast.158, ...), kind=kOutput, calls=%fused_computation.21.clone.1 | convolution fusion | flops 87293952 | bytes 897092 | tf_op jit(solution)/shard_map/while/body/eval_jaxpr/bmnj,bnrj->brm/dot_general | solution.py:134
  262.4 2.8 fusion.37
  266.5 4.0 %gather_fusion.2 = bf16[576,2048]{1,0:T(8,128)(2,1)} fusion(bf16[288,2048]{1,0:T(8,128)(2,1)S(1)} %pad_maximum_fusion, s32[1024]{0:T(1024)S(1)} %pad_clamp_fusion.3), kind=kCustom, calls=%fused_computation.2 | custom fusion | bytes 4720896 | tf_op jit(solution)/shard_map/jit(_take)/gather | solution.py:113
  270.4 11.7 %gather.23 = bf16[96,6,64,32]{3,2,1,0:T(8,128)(2,1)} reshape(bf16[576,2048]{1,0:T(8,128)(2,1)} %gather_fusion.2) | data formatting | bytes 4718592 | tf_op jit(solution)/shard_map/jit(_take)/gather | solution.py:113
  282.1 10.3 %bitcast_add_fusion.1 = f32[96,32,128]{2,1,0:T(8,128)} fusion(f32[12,8,32,128]{3,2,1,0:T(8,128)} %get-tuple-element.37, bf16[96,64,128]{2,1,0:T(8,128)(2,1)S(1)} %copy-done, f32[32,96,64]{2,0,1:T(8,128)S(1)} %copy-done.2, bf16[96,6,64,64]{3,2,1,0:T(8,128)(2,1)} %copy.71, bf16[96,6,64,32]{3,2,1,0:T(8,128)(2,1)} %gather.23, pred[96,6]{1,0:T(8,128)(4,1)S(1)} %copy-done.7, ...), kind=kOutput, calls=%fused_computation.44 | convolution fusion | flops 204472320 | bytes 12584640 | tf_op jit(solution)/shard_map/lkr,lkm->lrm/dot_general | solution.py:124
  (204 shorter events, 90.5 us)
Async XLA Ops:
  0.0 282.1 %copy-start = (bf16[96,64,128]{2,1,0:T(8,128)(2,1)S(1)}, bf16[96,64,128]{2,1,0:T(8,128)(2,1)}, u32[]{:S(2)}) copy-start(bf16[96,64,128]{2,1,0:T(8,128)(2,1)} %param.25) | copy-start | bytes 4718596
  4.9 260.2 %collective-permute-start.1 = (bf16[96,2048]{1,0:T(8,128)(2,1)}, bf16[96,2048]{1,0:T(8,128)(2,1)}, u32[]{:S(2)}, u32[]{:S(2)}) collective-permute-start(bf16[96,2048]{1,0:T(8,128)(2,1)} %copy.66), channel_id=1, source_target_pairs={{1,0},{2,1},{3,2},{4,3},{5,4},{6,5},{7,6},{8,7},{9,8},{10,9},{11,1... | collective-permute-start | bytes 1179656 | tf_op jit(solution)/shard_map/ppermute | solution.py:23
  14.2 250.9 %collective-permute-start = (bf16[96,2048]{1,0:T(8,128)(2,1)}, bf16[96,2048]{1,0:T(8,128)(2,1)}, u32[]{:S(2)}, u32[]{:S(2)}) collective-permute-start(bf16[96,2048]{1,0:T(8,128)(2,1)} %copy.66), channel_id=1, source_target_pairs={{0,1},{1,2},{2,3},{3,4},{4,5},{5,6},{6,7},{7,8},{8,9},{9,10},{10,1... | collective-permute-start | bytes 1179656 | tf_op jit(solution)/shard_map/ppermute | solution.py:21
  16.9 97.5 %collective-permute-start.4 = (bf16[4,32,128]{2,1,0:T(8,128)(2,1)S(1)}, bf16[4,32,128]{2,1,0:T(8,128)(2,1)S(1)}, u32[]{:S(2)}, u32[]{:S(2)}) collective-permute-start(bf16[4,32,128]{2,1,0:T(8,128)(2,1)S(1)} %get-tuple-element.80), channel_id=1, source_target_pairs={{0,1},{1,2},{2,3},{3,4},{4,5},{5,6},{6,7},{7,8},{8,9},{9,10},{10,1... | collective-permute-start | bytes 98312 | tf_op jit(solution)/shard_map/ppermute | solution.py:21
  20.0 87.0 %collective-permute-start.6 = (f32[4,7,128]{2,1,0:T(8,128)S(1)}, f32[4,7,128]{2,1,0:T(8,128)S(1)}, u32[]{:S(2)}, u32[]{:S(2)}) collective-permute-start(f32[4,7,128]{2,1,0:T(8,128)S(1)} %get-tuple-element.82), channel_id=1, source_target_pairs={{0,1},{1,2},{2,3},{3,4},{4,5},{5,6},{6,7},{7,8},{8,9},{9,10},{10,1... | collective-permute-start | bytes 43016 | tf_op jit(solution)/shard_map/ppermute | solution.py:21
  22.0 13.9 %copy-start.6 = (bf16[1,64,64]{2,1,0:T(8,128)(2,1)S(1)}, bf16[1,64,64]{2,1,0:T(8,128)(2,1)}, u32[]{:S(2)}) copy-start(bf16[1,64,64]{2,1,0:T(8,128)(2,1)} %param.31) | copy-start | bytes 24580
  22.0 89.0 %collective-permute-start.7 = (f32[4,7,128]{2,1,0:T(8,128)S(1)}, f32[4,7,128]{2,1,0:T(8,128)S(1)}, u32[]{:S(2)}, u32[]{:S(2)}) collective-permute-start(f32[4,7,128]{2,1,0:T(8,128)S(1)} %get-tuple-element.83), channel_id=1, source_target_pairs={{1,0},{2,1},{3,2},{4,3},{5,4},{6,5},{7,6},{8,7},{9,8},{10,9},{11,1... | collective-permute-start | bytes 43016 | tf_op jit(solution)/shard_map/ppermute | solution.py:23
  33.8 34.7 %copy-start.11 = (s32[1,6]{1,0:T(1,128)S(1)}, s32[1,6]{1,0:T(1,128)}, u32[]{:S(2)}) copy-start(s32[1,6]{1,0:T(1,128)} %param.34) | copy-start | bytes 76
  33.9 35.4 %copy-start.12 = (s32[1,6]{1,0:T(1,128)S(1)}, s32[1,6]{1,0:T(1,128)}, u32[]{:S(2)}) copy-start(s32[1,6]{1,0:T(1,128)} %param.38) | copy-start | bytes 76
  33.9 37.1 %copy-start.8 = (s32[96,6]{0,1:T(8,128)S(1)}, s32[96,6]{0,1:T(8,128)}, u32[]{:S(2)}) copy-start(s32[96,6]{0,1:T(8,128)} %param.29) | copy-start | bytes 6916
  33.9 37.9 %copy-start.10 = (s32[96]{0:T(128)S(1)}, s32[96]{0:T(128)}, u32[]{:S(2)}) copy-start(s32[96]{0:T(128)} %param.30) | copy-start | bytes 1156
  33.9 38.5 %copy-start.9 = (s32[96,8]{0,1:T(8,128)S(1)}, s32[96,8]{0,1:T(8,128)}, u32[]{:S(2)}) copy-start(s32[96,8]{0,1:T(8,128)} %param.23) | copy-start | bytes 9220
  62.9 190.4 %all-to-all-start = ((bf16[32,2,1024]{2,1,0:T(2,128)(2,1)}), bf16[32,2,1024]{2,1,0:T(2,128)(2,1)}, u32[]{:S(2)}, u32[]{:S(2)}) async-start(bf16[32,2,1024]{2,1,0:T(2,128)(2,1)} %reshape.251), calls=%async_computation | async-start | bytes 262144 | tf_op jit(solution)/shard_map/all_to_all | solution.py:90
  107.0 10.1 %collective-permute-start.5 = (bf16[4,32,128]{2,1,0:T(8,128)(2,1)S(1)}, bf16[4,32,128]{2,1,0:T(8,128)(2,1)S(1)}, u32[]{:S(2)}, u32[]{:S(2)}) collective-permute-start(bf16[4,32,128]{2,1,0:T(8,128)(2,1)S(1)} %get-tuple-element.81), channel_id=1, source_target_pairs={{1,0},{2,1},{3,2},{4,3},{5,4},{6,5},{7,6},{8,7},{9,8},{10,9},{11,1... | collective-permute-start | bytes 98312 | tf_op jit(solution)/shard_map/ppermute | solution.py:23
  111.0 138.1 %collective-permute-start.3 = (bf16[8,2048]{1,0:T(8,128)(2,1)}, bf16[8,2048]{1,0:T(8,128)(2,1)}, u32[]{:S(2)}, u32[]{:S(2)}) collective-permute-start(bf16[8,2048]{1,0:T(8,128)(2,1)} %bitcast.123), channel_id=1, source_target_pairs={{8,0},{16,8},{24,16},{32,24},{40,32},{48,40},{56,48},{64,56},{72,6... | collective-permute-start | bytes 98312 | tf_op jit(solution)/shard_map/ppermute | solution.py:23
  114.4 134.6 %collective-permute-start.2 = (bf16[8,2048]{1,0:T(8,128)(2,1)}, bf16[8,2048]{1,0:T(8,128)(2,1)}, u32[]{:S(2)}, u32[]{:S(2)}) collective-permute-start(bf16[8,2048]{1,0:T(8,128)(2,1)} %bitcast.123), channel_id=1, source_target_pairs={{0,8},{8,16},{16,24},{24,32},{32,40},{40,48},{48,56},{56,64},{64,7... | collective-permute-start | bytes 98312 | tf_op jit(solution)/shard_map/ppermute | solution.py:21
  249.1 10.9 %copy-start.13 = (pred[6]{0:T(512)(128)(4,1)S(1)}, pred[6]{0:T(512)(128)(4,1)}, u32[]{:S(2)}) copy-start(pred[6]{0:T(512)(128)(4,1)} %compare_and_fusion.2) | copy-start | bytes 22
  249.1 13.3 %copy-start.1 = (bf16[96,64,64]{2,1,0:T(8,128)(2,1)S(1)}, bf16[96,64,64]{2,1,0:T(8,128)(2,1)}, u32[]{:S(2)}) copy-start(bf16[96,64,64]{2,1,0:T(8,128)(2,1)} %copy.78) | copy-start | bytes 2359300
  255.4 7.0 %copy-start.3 = (f32[32,64]{1,0:T(8,128)S(1)}, f32[32,64]{1,0:T(8,128)}, u32[]{:S(2)}) copy-start(f32[32,64]{1,0:T(8,128)} %convolution_bitcast_fusion.3) | copy-start | bytes 24580
  255.4 7.0 %copy-start.5 = (bf16[1,64,64]{2,1,0:T(8,128)(2,1)S(1)}, bf16[1,64,64]{2,1,0:T(8,128)(2,1)}, u32[]{:S(2)}) copy-start(bf16[1,64,64]{2,1,0:T(8,128)(2,1)} %param.32) | copy-start | bytes 24580
  270.4 11.7 %copy-start.2 = (f32[32,96,64]{2,0,1:T(8,128)S(1)}, f32[32,96,64]{2,0,1:T(8,128)}, u32[]{:S(2)}) copy-start(f32[32,96,64]{2,0,1:T(8,128)} %fusion.37) | copy-start | bytes 2359300
  270.4 11.7 %copy-start.4 = (bf16[96,6]{1,0:T(8,128)(2,1)S(1)}, bf16[96,6]{1,0:T(8,128)(2,1)}, u32[]{:S(2)}) copy-start(bf16[96,6]{1,0:T(8,128)(2,1)} %fusion.49) | copy-start | bytes 3460
  270.4 11.7 %copy-start.7 = (pred[96,6]{1,0:T(8,128)(4,1)S(1)}, pred[96,6]{1,0:T(8,128)(4,1)}, u32[]{:S(2)}) copy-start(pred[96,6]{1,0:T(8,128)(4,1)} %copy.64) | copy-start | bytes 1732
